TPU v7x, 128 devices: a whole 4x4x4 slice. The times are simulated.
128 devices in a mesh: segment: 2 (over x_hi), blk: 64 (over y, z, x_lo, core).
Axes of the slice: x: 4 (x_hi: 2, x_lo: 2; x = x_hi * 2 + x_lo), y: 4, z: 4, core: 2. Of those that a mesh axis runs over, the one named last changes fastest.
Arguments:
- slabs: bfloat16 [32, 2048, 2048], P(None, 'blk'), may hold values from -6 to 6
- orbitals: bfloat16 [2048, 1024], P('blk'), may hold values from -0.125 to 0.125
- channel_orbital: int32 [1024], replicated, may hold values from 0 to 1023
- channel_target: int32 [1024], replicated, may hold values from 0 to 15
- coupling: int32 [16, 16], replicated, may hold values from -16 to 16
Outputs:
- channel_block: bfloat16 [32, 1024, 1024], P(None, 'blk', 'segment')
All inputs are finite; a program needn't handle non-finite values.
Results may differ from a plain program's by a relative error of at most 0.0056.
Values may be sent and summed in bfloat16 or wider, within the bound.
A program may use at most 64 MiB of HBM per device.

v0:
```python
import jax
import jax.numpy as jnp
from jax import lax
from jax.experimental import pallas as pl
from jax.experimental.pallas import tpu as pltpu
from jax.sharding import PartitionSpec as P

SIDE = 4
PIECES = 2
RINGED = ((), (1, 3))
EARLY = (1,)
FIRSTS = ((0, 1), (0, 3), (1, 1), (1, 3), (0, 2), (1, 2))
LASTS = ()
LATE = 0
NEAR = (0, 3, 1, 2, 5, 6, 4, 7)
DIMS = (((1,), (1,)), ((), ()))


def shifted(step):
    return jnp.where(step == 0, 2, jnp.where(step == 1, 1, jnp.where(step == 2, 3, 0)))


def body(
    slabs_ref, orbitals_ref, channel_ref, target_ref, coupling_ref,
    out_ref, angular_ref,
    slab_v, orb_v, channel_v, target_v, coupling_v, own, c, ct, half, panel, quarter,
    load_sem, near_send, near_recv, far_send, far_recv, sib_send, sib_recv,
    cross_send, cross_recv, other_send, other_recv, over_send, over_recv,
    swap_send, swap_recv, back_send, back_recv, own_sem,
):
    slabs, rows, depth = slab_v.shape
    blocks = depth // rows
    nch = ct.shape[0]
    cols = nch // 2
    part = cols // 2
    w = part // PIECES
    share = nch // blocks
    per_y = blocks // SIDE

    seg = lax.axis_index("segment")
    me = lax.axis_index("blk")
    core = me % 2
    pair = (me // 2) % 2
    z = (me // 4) % SIDE
    y = me // (4 * SIDE)
    sib = me + 1 - 2 * core
    across = me + 2 - 4 * pair
    cross = {"blk": across, "segment": 1 - seg}
    a = y * (1 - core) + z * core
    b = z * (1 - core) + y * core

    def at(da, dx, db, flip=0):
        spot = ((a + da) % SIDE) * (4 - 3 * core) + ((b + db) % SIDE) * (1 + 3 * core)
        return spot * 4 + ((pair + dx) % 2) * 2 + (core + flip) % 2

    loads = [
        pltpu.make_async_copy(src, dst, load_sem.at[i])
        for i, (src, dst) in enumerate([
            (channel_ref, channel_v), (orbitals_ref, orb_v), (target_ref, target_v),
            (coupling_ref, coupling_v), (slabs_ref, slab_v),
        ])
    ]
    for load in loads:
        load.start()

    near = [(0, 0), (1, 0), (3, 0), (0, 1), (2, 0), (1, 1), (3, 1), (2, 1)]
    partners = [at(da, dx, 0) for da, dx in near[1:]] + [at(da, dx, 0, 1) for da, dx in near]
    partners += [at(0, dx, db, 1) for db, dx in near if db] + [at(0, 0, db) for db in range(1, SIDE)]
    barrier = pltpu.get_barrier_semaphore()
    for partner in partners:
        pl.semaphore_signal(barrier, inc=1, device_id={"blk": partner})
    pl.semaphore_signal(barrier, inc=1, device_id=cross)

    def group(k, which, j, db):
        at_b = (b + db) % SIDE
        return c.at[which, 0, j, :, at_b] if k == 0 else c.at[which, 1, j, at_b]

    def chip(which, j, da, dx):
        pa = (a + da) % SIDE
        return c.at[which, core, j, pa * (1 - core) + b * core, b * (1 - core) + pa * core, (pair + dx) % 2]

    def each_core(do):
        for k in range(2):
            @pl.when(core == k)
            def _():
                do(k)

    def send(view, send_sem, recv_sem, device, dst=None):
        device = device if isinstance(device, dict) else {"blk": device}
        pltpu.make_async_remote_copy(
            src_ref=view, dst_ref=view if dst is None else dst,
            send_sem=send_sem, recv_sem=recv_sem, device_id=device,
        ).start()

    def arrived(sem, count):
        view = panel.at[0, pl.ds(0, count * rows), :]
        pltpu.make_async_copy(view, view, sem).wait()

    def make(j):
        picks = [
            channel_v[:, pl.ds(pl.multiple_of(seg * cols + (q * part + j * w), w), w)] for q in range(2)
        ]
        picks = jnp.concatenate(picks, axis=1)
        kinds = lax.broadcasted_iota(jnp.int32, (mine.shape[1], 2 * w), 0)
        onehot = jnp.where(kinds == picks, 1.0, 0.0).astype(jnp.bfloat16)
        got = jnp.dot(mine, onehot, preferred_element_type=jnp.float32).astype(jnp.bfloat16)
        for q in range(2):
            own[j, q] = got[:, q * w : (q + 1) * w]
        c[seg, core, j, y, z, pair, core] = own[j, core]

    def near_out(j):
        for i in NEAR:
            da, dx = near[i]
            recv = near_recv.at[j, i]
            if i:
                send(own.at[j, core], near_send.at[j], recv, at(da, dx, 0), c.at[seg, core, j, y, z, pair, core])
            send(
                own.at[j, 1 - core], near_send.at[j], recv, at(0, dx, da, 1),
                c.at[seg, 1 - core, j, y, z, pair, core],
            )

    def near_in(j):
        for i in NEAR:
            da, dx = near[i]
            arrived(near_recv.at[j, i], 2 if i else 1)
            view = chip(seg, j, -da, dx)
            for far in (2, 1, 3):
                send(view, far_send.at[j], far_recv.at[j, far - 1], at(0, 0, far))
            send(view, cross_send.at[j], cross_recv.at[j, 0], cross)
        each_core(lambda k: send(group(k, seg, j, 0), sib_send.at[j], sib_recv.at[j], sib))

    def far_in(j):
        for db in (1, 3, 2):
            arrived(far_recv.at[j, db - 1], 16)

            def do(k):
                view = group(k, seg, j, -db)
                send(view, sib_send.at[j], sib_recv.at[j], sib)
                if db not in RINGED[j]:
                    send(view, cross_send.at[j], cross_recv.at[j, db], cross)

            each_core(do)

    def other_in(j, db):
        arrived(other_recv.at[j, db - 1] if db in RINGED[j] else cross_recv.at[j, db], 16)

        def do(k):
            view = group(k, 1 - seg, j, -db)
            if db == 0:
                for far in RINGED[j]:
                    send(view, other_send.at[j], other_recv.at[j, far - 1], at(0, 0, far))
            send(view, over_send.at[j], over_recv.at[j], sib)

        each_core(do)

    def first(q, j):
        my_rows = pl.ds(pl.multiple_of(me * rows, rows), rows)

        def one(step, carry):
            at_y = (y + shifted(step)) % SIDE
            count = slabs // SIDE
            left = slab_v[pl.ds(at_y * count, count)].reshape(count * rows, depth)
            got = jnp.dot(left, c[seg, q, j].reshape(depth, w), preferred_element_type=jnp.float32)
            half[q, j, pl.ds(at_y * count, count)] = got.astype(jnp.bfloat16).reshape(count, rows, w)

            def go(i, carry):
                slab = at_y * count + (me // 2 + i) % count
                peer = slab * 2 + q

                @pl.when(peer != me)
                def _():
                    send(half.at[q, j, slab], swap_send.at[j], swap_recv.at[j], peer, panel.at[j, my_rows, :])

                return carry

            return lax.fori_loop(0, count, go, carry)

        lax.fori_loop(0, SIDE, one, 0)

    def turn(which):
        def one(i, carry):
            start = pl.multiple_of(i * 256, 256)
            for q in range(2):
                for j in range(PIECES):
                    top = pl.multiple_of(which * cols + (q * part + j * w), w)
                    piece = c[which, q, j, i // 2, pl.ds(i % 2 * 2, 2)].reshape(256, w)
                    ct[pl.ds(top, w), pl.ds(start, 256)] = piece.T
            return carry

        lax.fori_loop(0, depth // 256, one, 0)

    loads[0].wait()
    loads[1].wait()
    mine = orb_v[...]
    make(0)
    pl.semaphore_wait(barrier, len(partners) + 1)
    near_out(0)
    make(1)
    near_out(1)
    near_in(0)
    near_in(1)
    far_in(0)
    loads[4].wait()
    first(core, 0)
    for j in EARLY:
        other_in(j, 0)
    arrived(sib_recv.at[0], blocks)
    first(1 - core, 0)
    far_in(1)
    first(core, 1)
    arrived(sib_recv.at[1], blocks)
    first(1 - core, 1)
    for j in range(PIECES):
        panel[j, pl.ds(pl.multiple_of(me * rows, rows), rows), :] = half[core, j, me // 2]
    turn(seg)

    loads[2].wait()
    loads[3].wait()
    nt = coupling_v.shape[0]
    kinds = lax.broadcasted_iota(jnp.int32, (nt, nch), 0)
    hot = jnp.where(kinds == target_v[...], 1.0, 0.0).astype(jnp.bfloat16)
    channel = lax.broadcasted_iota(jnp.int32, (share, nch), 1)
    line = lax.broadcasted_iota(jnp.int32, (share, nch), 0)
    pick = jnp.where(channel == line + me * share, 1.0, 0.0).astype(jnp.bfloat16)
    hot_rows = lax.dot_general(pick, hot, DIMS, preferred_element_type=jnp.float32).astype(jnp.bfloat16)
    table = coupling_v[...].astype(jnp.float32).astype(jnp.bfloat16)
    mixed = jnp.dot(hot_rows, table, preferred_element_type=jnp.float32).astype(jnp.bfloat16)
    angular = jnp.dot(mixed, hot, preferred_element_type=jnp.float32) * (1.0 / 16.0)
    angular_ref[...] = jnp.where(seg == 0, angular[:, :cols], angular[:, cols:])

    for j in range(PIECES):
        if j not in EARLY:
            other_in(j, 0)
    for j, db in FIRSTS:
        other_in(j, db)

    def out_at(j):
        return out_ref.at[me // 2, :, pl.ds(pl.multiple_of(core * part + j * w, w), w)]

    def second(j, which):
        def one(step, carry):
            at_y = 2 * which + (y + 1 + step) % 2
            count = nch // SIDE
            left = ct[pl.ds(pl.multiple_of(at_y * count, count), count), :]
            got = jnp.dot(left, panel[j], preferred_element_type=jnp.float32).astype(jnp.bfloat16)
            quarter[j, pl.ds(at_y * per_y, per_y)] = got.reshape(per_y, share, w)

            def go(i, carry):
                peer = at_y * per_y + (me + i) % per_y

                @pl.when(peer != me)
                def _():
                    send(quarter.at[j, peer], back_send.at[j], back_recv.at[j], peer, out_at(j))

                return carry

            return lax.fori_loop(0, per_y, go, carry)

        lax.fori_loop(0, SIDE // 2, one, 0)

    arrived(swap_recv.at[0], blocks - 1)
    second(0, seg)
    if LATE:
        pass
        arrived(swap_recv.at[1], blocks - 1)
        second(1, seg)
    for j, db in LASTS:
        other_in(j, db)
    for j in range(PIECES):
        arrived(over_recv.at[j], blocks)
    turn(1 - seg)
    second(0, 1 - seg)
    if not LATE:
        pass
        arrived(swap_recv.at[1], blocks - 1)
        second(1, seg)
    second(1, 1 - seg)
    kept = [pltpu.make_async_copy(quarter.at[j, me], out_at(j), own_sem.at[j]) for j in range(PIECES)]
    for copy in kept:
        copy.start()
    for copy in kept:
        copy.wait()

    for j in range(PIECES):
        last = quarter.at[j, pl.ds(0, blocks - 1)]
        arrived(near_send.at[j], 15)
        arrived(far_send.at[j], 48)
        arrived(sib_send.at[j], blocks)
        arrived(cross_send.at[j], 16 * (4 - len(RINGED[j])))
        if RINGED[j]:
            arrived(other_send.at[j], 16 * len(RINGED[j]))
        arrived(over_send.at[j], blocks)
        arrived(swap_send.at[j], blocks - 1)
        pltpu.make_async_copy(last, last, back_send.at[j]).wait()
        pltpu.make_async_copy(last, last, back_recv.at[j]).wait()


def on_device(slabs, orbitals, channel_orbital, channel_target, coupling):
    blocks = lax.axis_size("blk")
    count, rows, depth = slabs.shape
    nch = channel_orbital.shape[0]
    cols = nch // 2
    part = cols // 2
    w = part // PIECES
    share = nch // blocks
    hbm = pl.BlockSpec(memory_space=pltpu.HBM)
    dma = pltpu.SemaphoreType.DMA
    each = dma((PIECES,))
    vmem = pltpu.VMEM
    picked, angular = pl.pallas_call(
        body,
        out_shape=(
            jax.ShapeDtypeStruct((count, share, cols), jnp.bfloat16),
            jax.ShapeDtypeStruct((share, cols), jnp.float32),
        ),
        in_specs=[hbm] * 5,
        out_specs=(pl.BlockSpec(memory_space=pl.ANY), pl.BlockSpec(memory_space=vmem)),
        scratch_shapes=[
            vmem((count, rows, depth), jnp.bfloat16),
            vmem(orbitals.shape, jnp.bfloat16),
            vmem((1, nch), jnp.int32),
            vmem((1, nch), jnp.int32),
            vmem(coupling.shape, jnp.int32),
            vmem((PIECES, 2, rows, w), jnp.bfloat16),
            vmem((2, 2, PIECES, SIDE, SIDE, 2, 2, rows, w), jnp.bfloat16),
            vmem((nch, depth), jnp.bfloat16),
            vmem((2, PIECES, count, rows, w), jnp.bfloat16),
            vmem((PIECES, depth, w), jnp.bfloat16),
            vmem((PIECES, blocks, share, w), jnp.bfloat16),
            dma((5,)), each, dma((PIECES, 8)), each, dma((PIECES, 3)), each, each,
            each, dma((PIECES, 4)), each, dma((PIECES, 3)), each, each,
            each, each, each, each, each,
        ],
        compiler_params=pltpu.CompilerParams(
            collective_id=0, has_side_effects=True, vmem_limit_bytes=48 * 1024 * 1024
        ),
        name="transform",
    )(*[
        pltpu.with_memory_space_constraint(v, pltpu.HBM)
        for v in (slabs, orbitals, channel_orbital.reshape(1, nch), channel_target.reshape(1, nch), coupling)
    ])
    return (angular[None] * picked.astype(jnp.float32)).astype(jnp.bfloat16)


def solution(mesh):
    return jax.shard_map(
        on_device,
        mesh=mesh,
        in_specs=(P(None, "blk", None), P("blk", None), P(), P(), P()),
        out_specs=P(None, "blk", "segment"),
        check_vma=False,
    )
```

profile of v0, /device:TPU:1, one launch (start us, length us, event | category | flops | bytes accessed | tf_op | source)
XLA Modules:
  0.0 44.0 jit_solution(8909559092419439501)
XLA Ops:
  0.0 43.1 %transform.1 = (bf16[32,16,512]{2,1,0:T(8,128)(2,1)S(1)}, f32[16,512]{1,0:T(8,128)S(1)}) custom-call(bf16[32,32,2048]{2,1,0:T(8,128)(2,1)} %slabs_ref.1, bf16[32,1024]{1,0:T(8,128)(2,1)} %orbitals_ref.1, s32[1,1024]{1,0:T(1,128)} %bitcast.2, s32[1,1024]{1,0:T(1,128)} %bitcast.3, s32[16,16]{1,0:T(8,128)} %coupling_ref.1), custom_call_target="tpu_custom_call" | custom-call | tf_op jit(solution)/shard_map/transform/pallas_call | solution.py:310
  43.1 0.9 %multiply_convert_fusion = bf16[32,16,512]{2,1,0:T(8,128)(2,1)} fusion(bf16[32,16,512]{2,1,0:T(8,128)(2,1)S(1)} %get-tuple-element.8, f32[16,512]{1,0:T(8,128)S(1)} %get-tuple-element.7), kind=kLoop, calls=%fused_computation | loop fusion | flops 786432 | bytes 1081344 | tf_op jit(solution)/shard_map/convert_element_type | solution.py:342
where the time goes:
time: 44.7 us; the launch traced here: 44 us
  Pallas kernels  43.1 us (96%)
  other arithmetic  0.91 us (2%)
    pallas_call x1, Pallas kernels, on_device(): pl.pallas_call(body, out_shape=(jax.ShapeDtypeStruct((count, share, cols)...  43.1 us
    convert_element_type x1, other arithmetic, on_device(): return (angular[None] * picked.astype(jnp.float32)).astype(jnp.bfloat16)  0.91 us

commit v1 on v0

--- a/solution.py
+++ b/solution.py
@@ -12,12 +12,9 @@
 FIRSTS = ((0, 1), (0, 3), (1, 1), (1, 3), (0, 2), (1, 2))
 LASTS = ()
 LATE = 0
+LAG = 1
 NEAR = (0, 3, 1, 2, 5, 6, 4, 7)
 DIMS = (((1,), (1,)), ((), ()))
-
-
-def shifted(step):
-    return jnp.where(step == 0, 2, jnp.where(step == 1, 1, jnp.where(step == 2, 3, 0)))
 
 
 def body(
@@ -149,7 +146,7 @@
             if db == 0:
                 for far in RINGED[j]:
                     send(view, other_send.at[j], other_recv.at[j, far - 1], at(0, 0, far))
-            send(view, over_send.at[j], over_recv.at[j], sib)
+            send(view, over_send.at[j], over_recv.at[j, db], sib)
 
         each_core(do)
 
@@ -157,7 +154,7 @@
         my_rows = pl.ds(pl.multiple_of(me * rows, rows), rows)
 
         def one(step, carry):
-            at_y = (y + shifted(step)) % SIDE
+            at_y = (y + step) % SIDE
             count = slabs // SIDE
             left = slab_v[pl.ds(at_y * count, count)].reshape(count * rows, depth)
             got = jnp.dot(left, c[seg, q, j].reshape(depth, w), preferred_element_type=jnp.float32)
@@ -176,6 +173,34 @@
             return lax.fori_loop(0, count, go, carry)
 
         lax.fori_loop(0, SIDE, one, 0)
+
+    def turn_group(q, j, db):
+        top = pl.multiple_of((1 - seg) * cols + (q * part + j * w), w)
+        if q == 0:
+            at_z = (z - db) % SIDE
+            for at_y in range(SIDE):
+                start = pl.multiple_of((at_y * SIDE + at_z) * 4 * rows, 4 * rows)
+                piece = c[1 - seg, 0, j, at_y, at_z].reshape(4 * rows, w)
+                ct[pl.ds(top, w), pl.ds(start, 4 * rows)] = piece.T
+        else:
+            at_y = (y - db) % SIDE
+            wide = SIDE * 4 * rows
+            piece = c[1 - seg, 1, j, at_y].reshape(wide, w)
+            ct[pl.ds(top, w), pl.ds(pl.multiple_of(at_y * wide, wide), wide)] = piece.T
+
+    def others(items, before=()):
+        waiting = list(before)
+        for j, db in items:
+            other_in(j, db)
+            each_core(lambda k: turn_group(k, j, db))
+            waiting.append((j, db))
+            if len(waiting) > LAG:
+                over_in(*waiting.pop(0))
+        return waiting
+
+    def over_in(j, db):
+        arrived(over_recv.at[j, db], 16)
+        each_core(lambda k: turn_group(1 - k, j, db))
 
     def turn(which):
         def one(i, carry):
@@ -204,6 +229,7 @@
     first(core, 0)
     for j in EARLY:
         other_in(j, 0)
+    waiting = [(j, 0) for j in EARLY]
     arrived(sib_recv.at[0], blocks)
     first(1 - core, 0)
     far_in(1)
@@ -228,11 +254,9 @@
     angular = jnp.dot(mixed, hot, preferred_element_type=jnp.float32) * (1.0 / 16.0)
     angular_ref[...] = jnp.where(seg == 0, angular[:, :cols], angular[:, cols:])
 
-    for j in range(PIECES):
-        if j not in EARLY:
-            other_in(j, 0)
-    for j, db in FIRSTS:
-        other_in(j, db)
+    for j in EARLY:
+        each_core(lambda k: turn_group(k, j, 0))
+    waiting = others([(j, 0) for j in range(PIECES) if j not in EARLY] + list(FIRSTS), waiting)
 
     def out_at(j):
         return out_ref.at[me // 2, :, pl.ds(pl.multiple_of(core * part + j * w, w), w)]
@@ -264,11 +288,8 @@
         pass
         arrived(swap_recv.at[1], blocks - 1)
         second(1, seg)
-    for j, db in LASTS:
-        other_in(j, db)
-    for j in range(PIECES):
-        arrived(over_recv.at[j], blocks)
-    turn(1 - seg)
+    for j, db in others(LASTS, waiting):
+        over_in(j, db)
     second(0, 1 - seg)
     if not LATE:
         pass
@@ -328,7 +349,7 @@
             vmem((PIECES, depth, w), jnp.bfloat16),
             vmem((PIECES, blocks, share, w), jnp.bfloat16),
             dma((5,)), each, dma((PIECES, 8)), each, dma((PIECES, 3)), each, each,
-            each, dma((PIECES, 4)), each, dma((PIECES, 3)), each, each,
+            each, dma((PIECES, 4)), each, dma((PIECES, 3)), each, dma((PIECES, 4)),
             each, each, each, each, each,
         ],
         compiler_params=pltpu.CompilerParams(

time: 44.7 us -> 43.4 us (0.971); the launches traced: 44 us -> 43.3 us
  Pallas kernels: 43.1 us -> 42.4 us
    pallas_call x1, Pallas kernels: 43.1 us -> 42.4 us  [on_device(): pl.pallas_call(body, out_shape=(jax.ShapeDtypeStruct((count, share, cols)...]
where the time goes in v1:
time: 43.4 us; the launch traced here: 43.3 us
  Pallas kernels  42.4 us (98%)
  other arithmetic  0.91 us (2%)
    pallas_call x1, Pallas kernels, on_device(): pl.pallas_call(body, out_shape=(jax.ShapeDtypeStruct((count, share, cols)...  42.4 us
    convert_element_type x1, other arithmetic, on_device(): return (angular[None] * picked.astype(jnp.float32)).astype(jnp.bfloat16)  0.91 us

profile of v1, /device:TPU:1, one launch (start us, length us, event | category | flops | bytes accessed | tf_op | source)
XLA Modules:
  0.0 43.3 jit_solution(2722130773233941754)
XLA Ops:
  0.0 42.4 %transform.1 = (bf16[32,16,512]{2,1,0:T(8,128)(2,1)S(1)}, f32[16,512]{1,0:T(8,128)S(1)}) custom-call(bf16[32,32,2048]{2,1,0:T(8,128)(2,1)} %slabs_ref.1, bf16[32,1024]{1,0:T(8,128)(2,1)} %orbitals_ref.1, s32[1,1024]{1,0:T(1,128)} %bitcast.2, s32[1,1024]{1,0:T(1,128)} %bitcast.3, s32[16,16]{1,0:T(8,128)} %coupling_ref.1), custom_call_target="tpu_custom_call" | custom-call | tf_op jit(solution)/shard_map/transform/pallas_call | solution.py:331
  42.4 0.9 %multiply_convert_fusion = bf16[32,16,512]{2,1,0:T(8,128)(2,1)} fusion(bf16[32,16,512]{2,1,0:T(8,128)(2,1)S(1)} %get-tuple-element.8, f32[16,512]{1,0:T(8,128)S(1)} %get-tuple-element.7), kind=kLoop, calls=%fused_computation | loop fusion | flops 786432 | bytes 1081344 | tf_op jit(solution)/shard_map/convert_element_type | solution.py:363

commit v2 on v1

--- a/solution.py
+++ b/solution.py
@@ -132,9 +132,9 @@
 
             def do(k):
                 view = group(k, seg, j, -db)
-                send(view, sib_send.at[j], sib_recv.at[j], sib)
                 if db not in RINGED[j]:
                     send(view, cross_send.at[j], cross_recv.at[j, db], cross)
+                send(view, sib_send.at[j], sib_recv.at[j], sib)
 
             each_core(do)
 
@@ -161,7 +161,7 @@
             half[q, j, pl.ds(at_y * count, count)] = got.astype(jnp.bfloat16).reshape(count, rows, w)
 
             def go(i, carry):
-                slab = at_y * count + (me // 2 + i) % count
+                slab = at_y * count + (me // 2 + 3 * i) % count
                 peer = slab * 2 + q
 
                 @pl.when(peer != me)
@@ -270,7 +270,7 @@
             quarter[j, pl.ds(at_y * per_y, per_y)] = got.reshape(per_y, share, w)
 
             def go(i, carry):
-                peer = at_y * per_y + (me + i) % per_y
+                peer = at_y * per_y + (me + 5 * i) % per_y
 
                 @pl.when(peer != me)
                 def _():

time: 43.4 us -> 43.3 us (level)
  no operation moved by 1% of the time
where the time goes in v2:
time: 43.3 us; the launch traced here: 43.2 us
  Pallas kernels  42.3 us (98%)
  other arithmetic  0.91 us (2%)
    pallas_call x1, Pallas kernels, on_device(): pl.pallas_call(body, out_shape=(jax.ShapeDtypeStruct((count, share, cols)...  42.3 us
    convert_element_type x1, other arithmetic, on_device(): return (angular[None] * picked.astype(jnp.float32)).astype(jnp.bfloat16)  0.91 us

profile of v2, /device:TPU:1, one launch (start us, length us, event | category | flops | bytes accessed | tf_op | source)
XLA Modules:
  0.0 43.2 jit_solution(9243026204913136779)
XLA Ops:
  0.0 42.3 %transform.1 = (bf16[32,16,512]{2,1,0:T(8,128)(2,1)S(1)}, f32[16,512]{1,0:T(8,128)S(1)}) custom-call(bf16[32,32,2048]{2,1,0:T(8,128)(2,1)} %slabs_ref.1, bf16[32,1024]{1,0:T(8,128)(2,1)} %orbitals_ref.1, s32[1,1024]{1,0:T(1,128)} %bitcast.2, s32[1,1024]{1,0:T(1,128)} %bitcast.3, s32[16,16]{1,0:T(8,128)} %coupling_ref.1), custom_call_target="tpu_custom_call" | custom-call | tf_op jit(solution)/shard_map/transform/pallas_call | solution.py:331
  42.3 0.9 %multiply_convert_fusion = bf16[32,16,512]{2,1,0:T(8,128)(2,1)} fusion(bf16[32,16,512]{2,1,0:T(8,128)(2,1)S(1)} %get-tuple-element.8, f32[16,512]{1,0:T(8,128)S(1)} %get-tuple-element.7), kind=kLoop, calls=%fused_computation | loop fusion | flops 786432 | bytes 1081344 | tf_op jit(solution)/shard_map/convert_element_type | solution.py:363
